TPU v7x, 32 devices: a whole 2x2x4 slice. The times are simulated.
32 devices in a mesh: tok: 16 (over z, x, core), head: 2 (over y).
Axes of the slice: x: 2, y: 2, z: 4, core: 2. Of those that a mesh axis runs over, the one named last changes fastest.
Arguments:
- queries: bfloat16 [1024, 4096], P('tok', 'head'), may hold values from -6 to 6
- keys: bfloat16 [8192, 1024], P('tok', 'head'), may hold values from -256 to 256
- values: bfloat16 [8192, 1024], P('tok', 'head'), may hold values from -6 to 6
- out_weight: bfloat16 [4096, 4096], P('head'), may hold values from -0.59765625 to 0.59765625
- task_slot: int32 [8, 8, 16], P('head'), may hold values from -1 to 7, as said below
- task_count: int32 [8, 16], P('head'), may hold values from 1 to 8, as said below
Outputs:
- projected: bfloat16 [1024, 4096], P('tok', 'head')
Inputs may be any that keep to these rules, and one draw needn't show every extreme that they name: For each key head h and key block c, the entries task_slot[h, b, c] that are not -1 take each of the values 0 to task_count[h, c] - 1 exactly once. Key blocks 0 and 15 are attended by every query block under every key head. task_count[h, c] is the number of query blocks that attend key block c under key head h.
All inputs are finite; a program needn't handle non-finite values.
Results may differ from a plain program's by a relative error of at most 0.015.
Values may be sent and summed in bfloat16 or wider, within the bound.
No kernel may reach another device: no remote copies, remote signals or barrier semaphores. Data moves between devices by JAX's collectives and lax.ppermute only.
A program may use at most 64 MiB of HBM per device.

v0:
```python
import jax
import jax.numpy as jnp
from jax import lax
from jax.sharding import PartitionSpec as P

HEADS = 32
KVH = 8
HEAD_SIZE = 128
QBLK = 128
theta_base = 500000.0
neg_fill = -1e30


def rotate(block_rows, first_row):
    head_width = block_rows.shape[-1]
    half_width = head_width // 2
    frequency = theta_base ** (-(jnp.arange(half_width, dtype=jnp.float32) * (2.0 / head_width)))
    places = (first_row + jnp.arange(block_rows.shape[0], dtype=jnp.int32)).astype(jnp.float32)
    angles = places[:, None] * frequency[None, :]
    cosine = jnp.cos(angles)[:, None, :]
    sine_table = jnp.sin(angles)[:, None, :]
    first_half = block_rows[..., :half_width]
    second_half = block_rows[..., half_width:]
    return jnp.concatenate(
        [
            first_half * cosine - second_half * sine_table,
            second_half * cosine + first_half * sine_table,
        ],
        axis=-1,
    )


def block_partial(query_row_block, head_keys_matrix, head_values_matrix):
    attention_logits = jnp.einsum(
        "qgd,kd->gqk", query_row_block, head_keys_matrix, preferred_element_type=jnp.float32
    ) * HEAD_SIZE ** (-0.5)
    maxima = jnp.max(attention_logits, axis=-1)
    probabilities = jnp.exp(attention_logits - maxima[..., None])
    totals = jnp.sum(probabilities, axis=-1)
    weighted_value_sum = jnp.einsum(
        "gqk,kd->qgd",
        probabilities.astype(jnp.bfloat16),
        head_values_matrix,
        preferred_element_type=jnp.float32,
    )
    normed = (weighted_value_sum / jnp.transpose(totals)[:, :, None]).astype(jnp.bfloat16)
    logsum = jnp.transpose(maxima + jnp.log(totals))
    return (normed, logsum)


def place_rows(buffers, cand_index, kv_local, row_start, normed, logsum):
    normed_all, logsum_all = buffers
    head_span = normed.shape[1]
    group_size = logsum.shape[1]
    column_normed = kv_local * head_span
    column_logsum = kv_local * group_size
    fresh_normed = normed[None]
    fresh_logsum = logsum[None]
    normed_all = lax.dynamic_update_slice(
        normed_all, fresh_normed, (cand_index, row_start, column_normed)
    )
    logsum_all = lax.dynamic_update_slice(
        logsum_all, fresh_logsum, (cand_index, row_start, column_logsum)
    )
    return (normed_all, logsum_all)


def column_at(task_slot, kv_local, server):
    return lax.dynamic_index_in_dim(task_slot[kv_local], server, 1, keepdims=False)


def count_at(task_count, kv_local, server):
    return lax.dynamic_index_in_dim(task_count[kv_local], server, 0, keepdims=False)


def run_slots(buffers, gathered, plan_entry, kv_local, group_size, blocks):
    cand_index, head_keys_matrix, head_values_matrix, column, range_low, range_high = plan_entry
    head_span = group_size * HEAD_SIZE
    block_ids = jnp.arange(blocks, dtype=jnp.int32)
    matches = column[:, None] == block_ids[None, :]
    lookup = jnp.sum(jnp.where(matches, block_ids[:, None], 0), axis=0)

    def step(slot_index, current):
        row_start = lookup[slot_index] * QBLK
        query_row_block = lax.dynamic_slice(
            gathered, (row_start, kv_local * head_span), (QBLK, head_span)
        ).reshape(QBLK, group_size, HEAD_SIZE)
        normed, logsum = block_partial(query_row_block, head_keys_matrix, head_values_matrix)
        return place_rows(
            current, cand_index, kv_local, row_start, normed.reshape(QBLK, head_span), logsum
        )

    return lax.fori_loop(range_low, range_high, step, buffers)


def on_device(queries, keys, values, out_weight, task_slot, task_count):
    servers = lax.axis_size("tok")
    server_index = lax.axis_index("tok")
    rows_dev = queries.shape[0]
    local_kv = task_slot.shape[0]
    blocks = task_slot.shape[1]
    group_size = HEADS // KVH
    head_span = group_size * HEAD_SIZE
    total_rows = rows_dev * servers
    shaped = queries.astype(jnp.float32).reshape(rows_dev, local_kv * group_size, HEAD_SIZE)
    rotated = (
        rotate(shaped, server_index * rows_dev)
        .astype(jnp.bfloat16)
        .reshape(rows_dev, local_kv * head_span)
    )
    task_plans = []
    for kv_local in range(local_kv):
        task_plans.append(
            [
                (
                    0,
                    keys[:, kv_local * HEAD_SIZE : (kv_local + 1) * HEAD_SIZE],
                    values[:, kv_local * HEAD_SIZE : (kv_local + 1) * HEAD_SIZE],
                    column_at(task_slot, kv_local, server_index),
                    jnp.int32(0),
                    count_at(task_count, kv_local, server_index),
                )
            ]
        )
    cand_total = 1
    initial = (
        jnp.zeros((cand_total, total_rows, local_kv * head_span), jnp.bfloat16),
        jnp.full((cand_total, total_rows, local_kv * group_size), neg_fill, jnp.float32),
    )
    gathered = lax.all_gather(rotated, "tok", axis=0, tiled=True)
    buffers = initial
    for kv_local in range(local_kv):
        for plan_entry in task_plans[kv_local]:
            buffers = run_slots(buffers, gathered, plan_entry, kv_local, group_size, blocks)
    normed_all, logsum_all = buffers
    back_normed = lax.all_to_all(normed_all[None], "tok", split_axis=2, concat_axis=0, tiled=True)
    back_logsum = lax.all_to_all(logsum_all[None], "tok", split_axis=2, concat_axis=0, tiled=True)
    sources = back_logsum.shape[0] * back_logsum.shape[1]
    logsum_recv = back_logsum.reshape(sources, rows_dev, local_kv * group_size)
    normed_recv = back_normed.reshape(sources, rows_dev, local_kv * group_size, HEAD_SIZE)
    largest = jnp.max(logsum_recv, axis=0)
    weights = jnp.exp(logsum_recv - largest[None])
    numerator = jnp.einsum("sqh,sqhd->qhd", weights, normed_recv.astype(jnp.float32))
    attention = (
        (numerator / jnp.sum(weights, axis=0)[:, :, None])
        .astype(jnp.bfloat16)
        .reshape(rows_dev, local_kv * head_span)
    )
    partial_out = jnp.dot(attention, out_weight, preferred_element_type=jnp.float32)
    return lax.psum_scatter(
        partial_out.astype(jnp.bfloat16), "head", scatter_dimension=1, tiled=True
    )


def solution(mesh):
    placed = (
        P("tok", "head"),
        P("tok", "head"),
        P("tok", "head"),
        P("head", None),
        P("head", None, None),
        P("head", None),
    )
    return jax.shard_map(
        on_device, mesh=mesh, in_specs=placed, out_specs=P("tok", "head"), check_vma=False
    )
```

profile of v0, /device:TPU:0, one launch (start us, length us, event | category | flops | bytes accessed | tf_op | source)
XLA Modules:
  0.0 463.4 jit_solution(422942893577546123)
XLA Ops:
  6.6 1.1 convert_bitcast_fusion
  11.9 50.7 %all-gather.2.cloned.1.call-done = bf16[1024,2048]{1,0:T(8,128)(2,1)} async-done(((bf16[64,2048]{1,0:T(8,128)(2,1)}), bf16[1024,2048]{1,0:T(8,128)(2,1)}) %all-gather.2.cloned.1.call-update) | async-done | bytes 4194320 | tf_op jit(solution)/shard_map/all_gather | solution.py:130
  62.7 6.4 %copy.78 = bf16[1024,2048]{0,1:T(8,128)(2,1)} copy(bf16[1024,2048]{1,0:T(8,128)(2,1)} %all-gather.2.cloned.1.call-done) | data formatting | bytes 8388608 | tf_op jit(solution)/shard_map/while | solution.py:93
  69.1 2.5 broadcast_in_dim.80
  71.5 38.5 %while.48 = (s32[]{:T(128)}, bf16[1,1024,2048]{1,2,0:T(8,128)(2,1)}, f32[1,1024,16]{1,2,0:T(8,128)S(1)}, s32[]{:T(128)}, s32[8]{0:T(128)S(1)}, /*index=5*/bf16[1...) while((s32[]{:T(128)}, ...), condition=%wide.region_4.5_spmd, body=%wide.region_1.4_spmd.sunk | while | flops 135921152 | bytes 4210925 | solution.py:93
  73.4 0.9 constant_dynamic-slice_fusion.12
  78.2 0.9 constant_dynamic-slice_fusion.12
  82.9 0.9 constant_dynamic-slice_fusion.12
  87.6 0.9 constant_dynamic-slice_fusion.12
  92.3 0.9 constant_dynamic-slice_fusion.12
  97.1 0.9 constant_dynamic-slice_fusion.12
  101.8 0.9 constant_dynamic-slice_fusion.12
  106.6 0.9 constant_dynamic-slice_fusion.12
  110.0 38.9 %while.49 = (s32[]{:T(128)}, bf16[1,1024,2048]{1,2,0:T(8,128)(2,1)}, f32[1,1024,16]{1,2,0:T(8,128)S(1)}, s32[]{:T(128)}, s32[8]{0:T(128)S(1)}, /*index=5*/bf16[1...) while((s32[]{:T(128)}, ...), condition=%wide.region_9.10_spmd, body=%wide.region_6.9_spmd.sunk | while | flops 135921152 | bytes 4210925 | solution.py:93
  112.0 0.9 constant_dynamic-slice_fusion.13
  116.8 0.9 constant_dynamic-slice_fusion.13
  121.5 0.9 constant_dynamic-slice_fusion.13
  126.3 0.9 constant_dynamic-slice_fusion.13
  131.1 0.9 constant_dynamic-slice_fusion.13
  135.9 0.9 constant_dynamic-slice_fusion.13
  140.7 0.9 constant_dynamic-slice_fusion.13
  145.4 0.9 constant_dynamic-slice_fusion.13
  149.0 38.4 %while.50 = (s32[]{:T(128)}, bf16[1,1024,2048]{1,2,0:T(8,128)(2,1)}, f32[1,1024,16]{1,2,0:T(8,128)S(1)}, s32[]{:T(128)}, s32[8]{0:T(128)S(1)}, /*index=5*/bf16[1...) while((s32[]{:T(128)}, ...), condition=%wide.region_14.15_spmd, body=%wide.region_11.14_spmd.sunk | while | flops 135921152 | bytes 4210925 | solution.py:93
  150.8 0.9 constant_dynamic-slice_fusion.14
  155.6 0.9 constant_dynamic-slice_fusion.14
  160.3 0.9 constant_dynamic-slice_fusion.14
  165.0 0.9 constant_dynamic-slice_fusion.14
  169.8 0.9 constant_dynamic-slice_fusion.14
  174.5 0.9 constant_dynamic-slice_fusion.14
  179.2 0.9 constant_dynamic-slice_fusion.14
  187.4 38.3 %while.51 = (s32[]{:T(128)}, bf16[1,1024,2048]{1,2,0:T(8,128)(2,1)}, f32[1,1024,16]{1,2,0:T(8,128)S(1)}, s32[]{:T(128)}, s32[8]{0:T(128)S(1)}, /*index=5*/bf16[1...) while((s32[]{:T(128)}, ...), condition=%wide.region_19.20_spmd, body=%wide.region_16.19_spmd.sunk | while | flops 135921152 | bytes 4210925 | solution.py:93
  193.9 0.9 constant_dynamic-slice_fusion.15
  198.7 0.9 constant_dynamic-slice_fusion.15
  222.2 0.9 constant_dynamic-slice_fusion.15
  226.5 2.0 reduce.10
  229.3 3.5 all-to-all-start
  232.8 20.7 %copy.89 = bf16[1,1,1024,2048]{3,1,0,2:T(2,128)(2,1)} copy(bf16[1,1,1024,2048]{2,3,1,0:T(8,128)(2,1)} %bitcast.233) | data formatting | bytes 8388608 | tf_op jit(solution)/shard_map/broadcast_in_dim | solution.py:136
  254.1 26.7 %reduce.12 = bf16[1024,2048]{1,0:T(8,128)(2,1)} reduce(bf16[1024,1,1,2048]{3,2,1,0:T(2,128)(2,1)} %bitcast.232, bf16[]{:T(256)} %broadcast.91), dimensions={1,2}, to_apply=%bitcast.126.reduce_sub_computation | reduce | bytes 8388610
  280.8 11.4 %reshape.171 = bf16[16,2,65536]{2,1,0:T(2,128)(2,1)} reshape(bf16[1024,2048]{1,0:T(8,128)(2,1)} %reduce.12) | data formatting | bytes 8388608
  292.2 6.0 %all-to-all-start.1 = ((bf16[16,2,65536]{2,1,0:T(2,128)(2,1)}), bf16[16,2,65536]{2,1,0:T(2,128)(2,1)}, u32[]{:S(2)}, u32[]{:S(2)}) async-start(bf16[16,2,65536]{2,1,0:T(2,128)(2,1)} %reshape.171), calls=%async_computation.1 | async-start | bytes 8388608 | tf_op jit(solution)/shard_map/all_to_all | solution.py:136
  299.3 0.9 reshape.170
  301.3 74.5 %all-to-all-done.1 = bf16[16,2,65536]{2,1,0:T(2,128)(2,1)} async-done(((bf16[16,2,65536]{2,1,0:T(2,128)(2,1)}), bf16[16,2,65536]{2,1,0:T(2,128)(2,1)}, u32[]{:S(2)}, u32[]{:S(2)}) %all-to-all-start.1) | async-done | bytes 4194336 | tf_op jit(solution)/shard_map/all_to_all | solution.py:136
  375.8 12.3 %reshape.172 = bf16[1024,1,1,2048]{3,2,1,0:T(2,128)(2,1)} reshape(bf16[16,2,65536]{2,1,0:T(2,128)(2,1)} %all-to-all-done.1) | data formatting | bytes 8388608
  388.1 24.7 %bitcast_reduce_fusion = bf16[1024,2048]{1,0:T(8,128)(2,1)S(1)} fusion(bf16[1024,1,1,2048]{3,2,1,0:T(2,128)(2,1)} %reshape.172), kind=kLoop, calls=%fused_computation.102 | loop fusion | bytes 8388608 | tf_op jit(solution)/shard_map/all_to_all | solution.py:136
  412.8 1.4 copy.106
  414.2 2.8 fusion.36
  417.2 9.6 %convolution_convert_fusion = bf16[64,4096]{1,0:T(8,128)(2,1)} fusion(bf16[2048,4096]{1,0:T(8,128)(2,1)} %param.17, bf16[8,8,16,128]{3,2,1,0:T(8,128)(2,1)S(1)} %bitcast.248), kind=kOutput, calls=%fused_computation.60 | convolution fusion | flops 1074003968 | bytes 17563648 | tf_op jit(solution)/shard_map/dot_general | solution.py:149
  426.8 29.8 %reduce-scatter.2.cloned.1.call-done = bf16[64,2048]{1,0:T(8,128)(2,1)} async-done(((bf16[64,4096]{1,0:T(8,128)(2,1)}), bf16[64,2048]{1,0:T(8,128)(2,1)}) %reduce-scatter.2.cloned.1.call-update) | async-done | bytes 262160 | tf_op jit(solution)/shard_map/reduce_scatter | solution.py:150
  (248 shorter events, 93.9 us)
Async XLA Ops:
  6.5 2.6 copy-start
  6.5 3.2 copy-start.3
  6.5 4.5 copy-start.2
  6.5 5.3 %copy-start.1 = (bf16[512,512]{1,0:T(8,128)(2,1)S(1)}, bf16[512,512]{1,0:T(8,128)(2,1)}, u32[]{:S(2)}) copy-start(bf16[512,512]{1,0:T(8,128)(2,1)} %param.15) | copy-start | bytes 1572868
  6.5 56.1 %all-gather.2.cloned.1.call-start = ((), (), s32[]{:S(2)}) async-start(), calls=%async_computation.3 | async-start | bytes 4456448 | tf_op jit(solution)/shard_map/all_gather | solution.py:130
  229.3 62.9 %all-to-all-start = ((f32[16,1,1024]{2,1,0:T(1,128)}), f32[16,1,1024]{2,1,0:T(1,128)S(1)}, u32[]{:S(2)}, u32[]{:S(2)}) async-start(f32[16,1,1024]{2,1,0:T(1,128)} %reshape.169), calls=%async_computation | async-start | bytes 131072 | tf_op jit(solution)/shard_map/all_to_all | solution.py:137
  292.2 83.6 %all-to-all-start.1 = ((bf16[16,2,65536]{2,1,0:T(2,128)(2,1)}), bf16[16,2,65536]{2,1,0:T(2,128)(2,1)}, u32[]{:S(2)}, u32[]{:S(2)}) async-start(bf16[16,2,65536]{2,1,0:T(2,128)(2,1)} %reshape.171), calls=%async_computation.1 | async-start | bytes 8388608 | tf_op jit(solution)/shard_map/all_to_all | solution.py:136
  298.2 158.3 %reduce-scatter.2.cloned.1.call-start = ((), (), s32[]{:S(2)}) async-start(), calls=%async_computation.4 | async-start | bytes 786432 | tf_op jit(solution)/shard_map/reduce_scatter | solution.py:150
Sparse Core Ops, SparseCore 0:
  9.5 53.0 all-gather.1
  426.9 29.5 reduce-scatter.1
where the time goes:
time: 466 us; the launch traced here: 463 us
  local copies, waits for them, and re-layouts  157 us (34%)
  waiting for transfers between devices  155 us (33%)
  loops' own time  45 us (10%)
  other arithmetic  43.2 us (9%)
  matrix products  39.9 us (9%)
  between operations  13.7 us (3%)
  starting transfers between devices  9.78 us (2%)
    all_to_all x1, waiting for transfers between devices, on_device(): lax.all_to_all(normed_all[None], 'tok', split_axis=2, concat_axis=0, tile...  74.5 us
    all_gather x1, waiting for transfers between devices, on_device(): gathered = lax.all_gather(rotated, 'tok', axis=0, tiled=True)  50.7 us
    another operation x4, loops' own time, run_slots(): return lax.fori_loop(range_low, range_high, step, buffers)  45 us
    unnamed x3, other arithmetic  29.8 us
    reduce_scatter x1, waiting for transfers between devices, on_device(): lax.psum_scatter(partial_out.astype(jnp.bfloat16), 'head', scatter_dimens...  29.8 us
    unnamed x21, local copies, waits for them, and re-layouts  29.4 us
    dynamic_slice x32, local copies, waits for them, and re-layouts, step(): lax.dynamic_slice(gathered, (row_start, kv_local * head_span), (QBLK, hea...  29.4 us
    all_to_all x1, local copies, waits for them, and re-layouts, on_device(): lax.all_to_all(normed_all[None], 'tok', split_axis=2, concat_axis=0, tile...  24.7 us
  transfers between devices with their start and end apart: 4, of which 3 were waited for; matrix products, arithmetic and copies ran while one was open for 14% of the time, Pallas kernels for 0%

commit v1 on v0

--- a/solution.py
+++ b/solution.py
@@ -133,7 +133,10 @@
         for plan_entry in task_plans[kv_local]:
             buffers = run_slots(buffers, gathered, plan_entry, kv_local, group_size, blocks)
     normed_all, logsum_all = buffers
-    back_normed = lax.all_to_all(normed_all[None], "tok", split_axis=2, concat_axis=0, tiled=True)
+    s0 = normed_all[None]
+    back_normed = jnp.concatenate(
+        lax.all_to_all(jnp.stack(jnp.split(s0, lax.psum(1, "tok"), 2)), "tok", 0, 0), 0
+    )
     back_logsum = lax.all_to_all(logsum_all[None], "tok", split_axis=2, concat_axis=0, tiled=True)
     sources = back_logsum.shape[0] * back_logsum.shape[1]
     logsum_recv = back_logsum.reshape(sources, rows_dev, local_kv * group_size)

time: 466 us -> 395 us (0.85)
  local copies, waits for them, and re-layouts: 157 us -> 115 us
  other arithmetic: 43.2 us -> 16.2 us
    unnamed x3 -> x2, other arithmetic: 29.8 us -> 2.93 us
    all_to_all x1 -> x0, local copies, waits for them, and re-layouts: 24.7 us -> none  [on_device(): lax.all_to_all(normed_all[None], 'tok', split_axis=2, concat_axis=0, tile...]
    broadcast_in_dim x1 -> x0, local copies, waits for them, and re-layouts: 20.7 us -> none  [on_device(): normed_all[None]]
    while x2 -> x3, local copies, waits for them, and re-layouts: 6.6 us -> 13.1 us  [run_slots(): return lax.fori_loop(range_low, range_high, step, buffers)]
    unnamed x21 -> x35, local copies, waits for them, and re-layouts: 29.4 us -> 25.8 us
  transfers between devices with their start and end apart: 4 -> 4, of which waited for: 3 -> 3; matrix products, arithmetic and copies ran while one was open for 14% -> 8% of each run, Pallas kernels for 0% -> 0%
where the time goes in v1:
time: 395 us; the launch traced here: 393 us
  waiting for transfers between devices  155 us (39%)
  local copies, waits for them, and re-layouts  115 us (29%)
  loops' own time  43 us (11%)
  matrix products  39.9 us (10%)
  other arithmetic  16.2 us (4%)
  between operations  13.7 us (3%)
  starting transfers between devices  9.78 us (2%)
    all_to_all x1, waiting for transfers between devices, on_device(): lax.all_to_all(jnp.stack(jnp.split(s0, lax.psum(1, 'tok'), 2)), 'tok', 0, 0)  74.6 us
    all_gather x1, waiting for transfers between devices, on_device(): gathered = lax.all_gather(rotated, 'tok', axis=0, tiled=True)  50.7 us
    another operation x4, loops' own time, run_slots(): return lax.fori_loop(range_low, range_high, step, buffers)  43 us
    reduce_scatter x1, waiting for transfers between devices, on_device(): lax.psum_scatter(partial_out.astype(jnp.bfloat16), 'head', scatter_dimens...  29.8 us
    dynamic_slice x32, local copies, waits for them, and re-layouts, step(): lax.dynamic_slice(gathered, (row_start, kv_local * head_span), (QBLK, hea...  29.4 us
    unnamed x35, local copies, waits for them, and re-layouts  25.8 us
    dynamic_update_slice x32, local copies, waits for them, and re-layouts, place_rows(): lax.dynamic_update_slice(normed_all, fresh_normed, (cand_index, row_start...  22 us
    dynamic_slice x32, local copies, waits for them, and re-layouts, step(): row_start = lookup[slot_index] * QBLK  18.8 us
  transfers between devices with their start and end apart: 4, of which 3 were waited for; matrix products, arithmetic and copies ran while one was open for 8% of the time, Pallas kernels for 0%

profile of v1, /device:TPU:0, one launch (start us, length us, event | category | flops | bytes accessed | tf_op | source)
XLA Modules:
  0.0 392.8 jit_solution(11951555893118960728)
XLA Ops:
  6.6 1.1 convert_bitcast_fusion
  11.9 50.7 %all-gather.2.cloned.1.call-done = bf16[1024,2048]{1,0:T(8,128)(2,1)} async-done(((bf16[64,2048]{1,0:T(8,128)(2,1)}), bf16[1024,2048]{1,0:T(8,128)(2,1)}) %all-gather.2.cloned.1.call-update) | async-done | bytes 4194320 | tf_op jit(solution)/shard_map/all_gather | solution.py:130
  62.6 6.4 %copy.59 = bf16[1024,2048]{0,1:T(8,128)(2,1)} copy(bf16[1024,2048]{1,0:T(8,128)(2,1)} %all-gather.2.cloned.1.call-done) | data formatting | bytes 8388608 | tf_op jit(solution)/shard_map/while | solution.py:93
  69.0 2.5 broadcast_in_dim.80
  71.5 38.4 %while.48 = (s32[]{:T(128)}, bf16[1,1024,2048]{1,2,0:T(8,128)(2,1)}, f32[1,1024,16]{1,2,0:T(8,128)S(1)}, s32[]{:T(128)}, s32[8]{0:T(128)S(1)}, /*index=5*/bf16[1...) while((s32[]{:T(128)}, ...), condition=%wide.region_4.5_spmd, body=%wide.region_1.4_spmd.sunk | while | flops 135921152 | bytes 4210925 | solution.py:93
  73.4 0.9 constant_dynamic-slice_fusion.12
  78.1 0.9 constant_dynamic-slice_fusion.12
  82.9 0.9 constant_dynamic-slice_fusion.12
  87.6 0.9 constant_dynamic-slice_fusion.12
  92.3 0.9 constant_dynamic-slice_fusion.12
  97.0 0.9 constant_dynamic-slice_fusion.12
  101.7 0.9 constant_dynamic-slice_fusion.12
  106.4 0.9 constant_dynamic-slice_fusion.12
  109.9 37.8 %while.49 = (s32[]{:T(128)}, bf16[1,1024,2048]{1,2,0:T(8,128)(2,1)}, f32[1,1024,16]{1,2,0:T(8,128)S(1)}, s32[]{:T(128)}, s32[8]{0:T(128)S(1)}, /*index=5*/bf16[1...) while((s32[]{:T(128)}, ...), condition=%wide.region_9.10_spmd, body=%wide.region_6.9_spmd.sunk | while | flops 135921152 | bytes 4210925 | solution.py:93
  111.7 0.9 constant_dynamic-slice_fusion.13
  116.4 0.9 constant_dynamic-slice_fusion.13
  121.0 0.9 constant_dynamic-slice_fusion.13
  125.7 0.9 constant_dynamic-slice_fusion.13
  130.4 0.9 constant_dynamic-slice_fusion.13
  135.0 0.9 constant_dynamic-slice_fusion.13
  139.7 0.9 constant_dynamic-slice_fusion.13
  144.3 0.9 constant_dynamic-slice_fusion.13
  147.7 38.0 %while.50 = (s32[]{:T(128)}, bf16[1,1024,2048]{1,2,0:T(8,128)(2,1)}, f32[1,1024,16]{1,2,0:T(8,128)S(1)}, s32[]{:T(128)}, s32[8]{0:T(128)S(1)}, /*index=5*/bf16[1...) while((s32[]{:T(128)}, ...), condition=%wide.region_14.15_spmd, body=%wide.region_11.14_spmd.sunk | while | flops 135921152 | bytes 4210925 | solution.py:93
  149.6 0.9 constant_dynamic-slice_fusion.14
  158.9 0.9 constant_dynamic-slice_fusion.14
  172.9 0.9 constant_dynamic-slice_fusion.14
  182.3 0.9 constant_dynamic-slice_fusion.14
  185.7 37.9 %while.51 = (s32[]{:T(128)}, bf16[1,1024,2048]{1,2,0:T(8,128)(2,1)}, f32[1,1024,16]{1,2,0:T(8,128)S(1)}, s32[]{:T(128)}, s32[8]{0:T(128)S(1)}, /*index=5*/bf16[1...) while((s32[]{:T(128)}, ...), condition=%wide.region_19.20_spmd, body=%wide.region_16.19_spmd.sunk | while | flops 135921152 | bytes 4210925 | solution.py:93
  210.9 0.9 constant_dynamic-slice_fusion.15
  215.6 0.9 constant_dynamic-slice_fusion.15
  224.4 1.9 reduce.8
  227.1 3.5 all-to-all-start
  230.6 6.5 %copy.69 = bf16[1,1024,2048]{2,1,0:T(8,128)(2,1)} copy(bf16[1,1024,2048]{1,2,0:T(8,128)(2,1)} %get-tuple-element.188) | data formatting | bytes 8388608 | tf_op jit(solution)/shard_map/while | solution.py:93
  237.1 1.8 fusion.55
  238.9 1.7 fusion.54
  240.6 1.7 fusion.53
  242.3 1.7 fusion.52
  244.0 1.7 fusion.51
  245.6 1.7 fusion.50
  247.3 1.7 fusion.49
  249.0 1.7 fusion.48
  256.5 6.0 %all-to-all-start.1 = ((bf16[16,1,1,64,2048]{4,3,2,1,0:T(8,128)(2,1)}), bf16[16,1,1,64,2048]{4,3,2,1,0:T(8,128)(2,1)}, u32[]{:S(2)}, u32[]{:S(2)}) async-start(bf16[16,1,1,64,2048]{4,3,2,1,0:T(8,128)(2,1)} %fusion.40), calls=%async_computation.1 | async-start | bytes 8388608 | tf_op jit(solution)/shard_map/all_to_all | solution.py:138
  263.4 0.9 reshape.161
  265.4 74.6 %all-to-all-done.1 = bf16[16,1,1,64,2048]{4,3,2,1,0:T(8,128)(2,1)} async-done(((bf16[16,1,1,64,2048]{4,3,2,1,0:T(8,128)(2,1)}), bf16[16,1,1,64,2048]{4,3,2,1,0:T(8,128)(2,1)}, u32[]{:S(2)}, u32[]{:S(2)}) %all-to-all-start.1) | async-done | bytes 4194336 | tf_op jit(solution)/shard_map/all_to_all | solution.py:138
  340.0 3.6 copy.84
  343.6 2.8 fusion.36
  346.6 9.6 %convolution_convert_fusion = bf16[64,4096]{1,0:T(8,128)(2,1)} fusion(bf16[2048,4096]{1,0:T(8,128)(2,1)} %param.17, bf16[8,8,16,128]{3,2,1,0:T(8,128)(2,1)S(1)} %bitcast.324), kind=kOutput, calls=%fused_computation.60 | convolution fusion | flops 1074003968 | bytes 17563648 | tf_op jit(solution)/shard_map/dot_general | solution.py:152
  356.3 29.8 %reduce-scatter.2.cloned.1.call-done = bf16[64,2048]{1,0:T(8,128)(2,1)} async-done(((bf16[64,4096]{1,0:T(8,128)(2,1)}), bf16[64,2048]{1,0:T(8,128)(2,1)}) %reduce-scatter.2.cloned.1.call-update) | async-done | bytes 262160 | tf_op jit(solution)/shard_map/reduce_scatter | solution.py:153
  (261 shorter events, 102.6 us)
Async XLA Ops:
  6.5 2.6 copy-start.1
  6.5 3.2 copy-start.4
  6.5 4.5 %copy-start.3 = (s32[4,8,16]{2,1,0:T(8,128)S(1)}, s32[4,8,16]{2,1,0:T(8,128)}, u32[]{:S(2)}) copy-start(s32[4,8,16]{2,1,0:T(8,128)} %param.18) | copy-start | bytes 6148
  6.5 5.3 %copy-start.2 = (bf16[512,512]{1,0:T(8,128)(2,1)S(1)}, bf16[512,512]{1,0:T(8,128)(2,1)}, u32[]{:S(2)}) copy-start(bf16[512,512]{1,0:T(8,128)(2,1)} %param.15) | copy-start | bytes 1572868
  6.5 56.1 %all-gather.2.cloned.1.call-start = ((), (), s32[]{:S(2)}) async-start(), calls=%async_computation.3 | async-start | bytes 4456448 | tf_op jit(solution)/shard_map/all_gather | solution.py:130
  227.1 29.4 %all-to-all-start = ((f32[16,1,1024]{2,1,0:T(1,128)}), f32[16,1,1024]{2,1,0:T(1,128)S(1)}, u32[]{:S(2)}, u32[]{:S(2)}) async-start(f32[16,1,1024]{2,1,0:T(1,128)} %reshape.160), calls=%async_computation | async-start | bytes 131072 | tf_op jit(solution)/shard_map/all_to_all | solution.py:140
  237.1 13.5 %copy-start = (bf16[1,1024,2048]{2,1,0:T(8,128)(2,1)S(1)}, bf16[1,1024,2048]{2,1,0:T(8,128)(2,1)}, u32[]{:S(2)}) copy-start(bf16[1,1024,2048]{2,1,0:T(8,128)(2,1)} %copy.69) | copy-start | bytes 12582916
  256.5 83.6 %all-to-all-start.1 = ((bf16[16,1,1,64,2048]{4,3,2,1,0:T(8,128)(2,1)}), bf16[16,1,1,64,2048]{4,3,2,1,0:T(8,128)(2,1)}, u32[]{:S(2)}, u32[]{:S(2)}) async-start(bf16[16,1,1,64,2048]{4,3,2,1,0:T(8,128)(2,1)} %fusion.40), calls=%async_computation.1 | async-start | bytes 8388608 | tf_op jit(solution)/shard_map/all_to_all | solution.py:138
  262.5 123.5 %reduce-scatter.2.cloned.1.call-start = ((), (), s32[]{:S(2)}) async-start(), calls=%async_computation.4 | async-start | bytes 786432 | tf_op jit(solution)/shard_map/reduce_scatter | solution.py:153
Sparse Core Ops, SparseCore 0:
  9.5 53.0 all-gather.1
  356.4 29.5 reduce-scatter.1
